TPU v7x, 32 devices: a whole 2x2x4 slice. The times are simulated.
32 devices in a mesh: gx: 4 (over y, x), gz: 8 (over z, core).
Axes of the slice: x: 2, y: 2, z: 4, core: 2. Of those that a mesh axis runs over, the one named last changes fastest.
Arguments:
- sources: float32 [8, 4, 8, 1280, 128], P('gz', 'gx'), may hold values from -6 to 6
- green: float32 [8, 4, 1280, 1280], P('gz', 'gx'), may hold values from -0.2 to 1.2
- probe: float32 [8, 4, 1024, 1280], P('gz', 'gx'), may hold values from -0.078125 to 0.078125
- batch_pick: int32 [8, 11], replicated, may hold values from 0 to 7
- owner_map: int32 [8, 512], P('gz'), may hold values from 0 to 511, each once within a row
Outputs:
- outgoing: float32 [8, 4, 1280, 1024], P('gz', 'gx')
- receiver_data: float32 [8, 2, 512, 1024], P('gz', None, 'gx')
Inputs may be any that keep to these rules, and one draw needn't show every extreme that they name: Each row of owner_map holds every receiver once; slot q belongs to the column q // (512 // 4).
All inputs are finite; a program needn't handle non-finite values.
Results may differ from a plain program's by a relative error of at most 0.00013.
Values sent between devices are 32-bit elements; how exact they have to be, the bound alone decides.
A program may use at most 128 MiB of HBM per device.

v0:
```python
import jax
import jax.numpy as jnp
from jax import lax
from jax.sharding import PartitionSpec as P


def passed_along(value, axis, steps):
    count = lax.axis_size(axis)
    first, last = (max(0, -steps), min(count, count - steps))
    return lax.ppermute(value, axis, [(source, source + steps) for source in range(first, last)])


def local(sources, green, probe, batch_pick, owner_map):
    column = lax.axis_index("gx")
    row = lax.axis_index("gz")
    diag = row + column
    operator = green[0, 0]
    local_sources = sources[0, 0]
    trace = operator.shape[0]
    shots = local_sources.shape[2]
    window = batch_pick.shape[0]
    total = window * shots
    units = total // shots
    steps = units + lax.axis_size("gx") + lax.axis_size("gz") - 2

    def advance(step, carry):
        upper, lefter, traces = carry
        unit = step - diag
        active = jnp.logical_and(unit >= 0, unit < units)
        start = jnp.clip(unit, 0, units - 1) * shots
        batch = start // shots
        chosen = batch_pick[batch, diag]
        source_set = lax.dynamic_index_in_dim(local_sources, chosen, 0, keepdims=False)

        def work(stored):
            inflow = source_set + 0.5 * (upper + lefter)
            result = jnp.dot(
                operator,
                inflow,
                precision=lax.Precision.HIGHEST,
                preferred_element_type=jnp.float32,
            )
            return (result, lax.dynamic_update_slice_in_dim(stored, result, start, 1))

        def skip(stored):
            return (jnp.zeros((trace, shots), jnp.float32), stored)

        result, traces = lax.cond(active, work, skip, traces)
        lower = passed_along(result, "gz", 1)
        righter = passed_along(result, "gx", 1)
        return (lower, righter, traces)

    blank = jnp.zeros((trace, shots), jnp.float32)
    start_traces = jnp.zeros((trace, total), jnp.float32)
    upper, lefter, traces = lax.fori_loop(0, steps, advance, (blank, blank, start_traces))
    partial_value = jnp.dot(
        probe[0, 0], traces, precision=lax.Precision.HIGHEST, preferred_element_type=jnp.float32
    )
    receivers = owner_map.shape[1]
    partial_value = partial_value.reshape(2, receivers, total)
    ordered = jnp.take(partial_value, owner_map[0], axis=1)
    shared = lax.psum_scatter(ordered, "gx", scatter_dimension=1, tiled=True)
    return (traces[None, None], shared[None])


def solution(mesh):
    return jax.shard_map(
        local,
        mesh=mesh,
        in_specs=(
            P("gz", "gx", None, None, None),
            P("gz", "gx", None, None),
            P("gz", "gx", None, None),
            P(),
            P("gz", None),
        ),
        out_specs=(P("gz", "gx", None, None), P("gz", None, "gx", None)),
        check_vma=False,
    )
```

profile of v0, /device:TPU:29, one launch (start us, length us, event | category | flops | bytes accessed | tf_op | source)
XLA Modules:
  0.0 683.8 jit_solution(969338325766610109)
XLA Ops:
  7.2 2.6 broadcast_in_dim.19
  10.0 504.1 %while.22 = (s32[]{:T(128)}, f32[1280,128]{0,1:T(8,128)S(1)}, f32[1280,128]{0,1:T(8,128)S(1)}, f32[1280,1024]{0,1:T(8,128)}, s32[]{:T(128)}, /*index=5*/s32[8,11...) while((s32[]{:T(128)}, f32[1280,128]{0,1:T(8,128)S(1)}, ...), condition=%wide.region_3.4_spmd, body=%wide.region_0.3_spmd.sunk | while | flops 2517073920 | bytes 18350752 | solution.py:55
  12.2 3.1 collective-permute-start.1
  15.3 14.8 %collective-permute-done.1 = f32[1280,128]{0,1:T(8,128)S(1)} collective-permute-done((f32[1280,128]{0,1:T(8,128)}, f32[1280,128]{0,1:T(8,128)S(1)}, u32[]{:S(2)}, u32[]{:S(2)}) %collective-permute-start.1) | collective-permute-done | bytes 655392 | tf_op jit(solution)/shard_map/while/body/eval_jaxpr/ppermute | solution.py:10
  32.3 2.2 collective-permute-start.1
  34.6 2.3 collective-permute-done
  36.9 11.9 %collective-permute-done.1 = f32[1280,128]{0,1:T(8,128)S(1)} collective-permute-done((f32[1280,128]{0,1:T(8,128)}, f32[1280,128]{0,1:T(8,128)S(1)}, u32[]{:S(2)}, u32[]{:S(2)}) %collective-permute-start.1) | collective-permute-done | bytes 655392 | tf_op jit(solution)/shard_map/while/body/eval_jaxpr/ppermute | solution.py:10
  51.0 1.9 collective-permute-start.1
  52.9 4.1 collective-permute-done
  57.0 9.0 %collective-permute-done.1 = f32[1280,128]{0,1:T(8,128)S(1)} collective-permute-done((f32[1280,128]{0,1:T(8,128)}, f32[1280,128]{0,1:T(8,128)S(1)}, u32[]{:S(2)}, u32[]{:S(2)}) %collective-permute-start.1) | collective-permute-done | bytes 655392 | tf_op jit(solution)/shard_map/while/body/eval_jaxpr/ppermute | solution.py:10
  68.2 1.9 collective-permute-start.1
  70.1 5.6 collective-permute-done
  75.7 6.0 collective-permute-done.1
  83.9 1.9 collective-permute-start.1
  85.8 7.1 %collective-permute-done = f32[1280,128]{0,1:T(8,128)S(1)} collective-permute-done((f32[1280,128]{0,1:T(8,128)}, f32[1280,128]{0,1:T(8,128)S(1)}, u32[]{:S(2)}, u32[]{:S(2)}) %collective-permute-start) | collective-permute-done | bytes 655392 | tf_op jit(solution)/shard_map/while/body/eval_jaxpr/ppermute | solution.py:10
  92.9 3.4 collective-permute-done.1
  98.5 1.9 collective-permute-start.1
  100.4 11.9 %collective-permute-done = f32[1280,128]{0,1:T(8,128)S(1)} collective-permute-done((f32[1280,128]{0,1:T(8,128)}, f32[1280,128]{0,1:T(8,128)S(1)}, u32[]{:S(2)}, u32[]{:S(2)}) %collective-permute-start) | collective-permute-done | bytes 655392 | tf_op jit(solution)/shard_map/while/body/eval_jaxpr/ppermute | solution.py:10
  114.5 1.9 collective-permute-start.1
  116.5 15.8 %collective-permute-done = f32[1280,128]{0,1:T(8,128)S(1)} collective-permute-done((f32[1280,128]{0,1:T(8,128)}, f32[1280,128]{0,1:T(8,128)S(1)}, u32[]{:S(2)}, u32[]{:S(2)}) %collective-permute-start) | collective-permute-done | bytes 655392 | tf_op jit(solution)/shard_map/while/body/eval_jaxpr/ppermute | solution.py:10
  134.5 1.9 collective-permute-start.1
  136.4 15.8 %collective-permute-done = f32[1280,128]{0,1:T(8,128)S(1)} collective-permute-done((f32[1280,128]{0,1:T(8,128)}, f32[1280,128]{0,1:T(8,128)S(1)}, u32[]{:S(2)}, u32[]{:S(2)}) %collective-permute-start) | collective-permute-done | bytes 655392 | tf_op jit(solution)/shard_map/while/body/eval_jaxpr/ppermute | solution.py:10
  154.4 1.9 collective-permute-start.1
  156.3 72.7 %collective-permute-done = f32[1280,128]{0,1:T(8,128)S(1)} collective-permute-done((f32[1280,128]{0,1:T(8,128)}, f32[1280,128]{0,1:T(8,128)S(1)}, u32[]{:S(2)}, u32[]{:S(2)}) %collective-permute-start) | collective-permute-done | bytes 655392 | tf_op jit(solution)/shard_map/while/body/eval_jaxpr/ppermute | solution.py:10
  229.0 16.3 %conditional.2 = (f32[1280,128]{0,1:T(8,128)}, f32[1280,1024]{0,1:T(8,128)}) conditional(s32[]{:T(128)} %convert_element_type.11, f32[1280,1024]{0,1:T(8,128)} %get-tuple-element.579, (s32[]{:T(128)}, pred[]{:T(512)}, pred[]{:T(512)}, s32[]{:T(128)}, s32[8,11]{1,0:T(8,128)}, /*index=5*/s32[]{:T(128)}, f32[8,1280,128]{2,1,0:T(8,128)}, ...), branch_computations={%region_1.1_spmd, %region_2.2_spmd.clone} | conditional | flops 2517073920 | bytes 13107479 | solution.py:48
  232.7 9.5 %convolution_bitcast_fusion = f32[1280,128]{0,1:T(8,128)} fusion(f32[1280,1280]{1,0:T(8,128)} %get-tuple-element.463, f32[1280,128]{1,0:T(8,128)S(1)} %copy.20, f32[1280,128]{1,0:T(8,128)S(1)} %copy.21, f32[8,1280,128]{2,1,0:T(8,128)} %get-tuple-element.460, s32[]{:T(128)S(6)} %select_n.86), kind=kOutput, calls=%fused_computation.1 | convolution fusion | flops 2517073920 | bytes 9175044 | tf_op jit(solution)/shard_map/while/body/eval_jaxpr/cond/branch_1_fun/dot_general | solution.py:37
  242.2 3.1 dynamic_update_slice.7
  248.5 12.4 %collective-permute-done = f32[1280,128]{0,1:T(8,128)S(1)} collective-permute-done((f32[1280,128]{0,1:T(8,128)}, f32[1280,128]{0,1:T(8,128)S(1)}, u32[]{:S(2)}, u32[]{:S(2)}) %collective-permute-start) | collective-permute-done | bytes 655392 | tf_op jit(solution)/shard_map/while/body/eval_jaxpr/ppermute | solution.py:10
  260.9 16.3 %conditional.2 = (f32[1280,128]{0,1:T(8,128)}, f32[1280,1024]{0,1:T(8,128)}) conditional(s32[]{:T(128)} %convert_element_type.11, f32[1280,1024]{0,1:T(8,128)} %get-tuple-element.579, (s32[]{:T(128)}, pred[]{:T(512)}, pred[]{:T(512)}, s32[]{:T(128)}, s32[8,11]{1,0:T(8,128)}, /*index=5*/s32[]{:T(128)}, f32[8,1280,128]{2,1,0:T(8,128)}, ...), branch_computations={%region_1.1_spmd, %region_2.2_spmd.clone} | conditional | flops 2517073920 | bytes 13107479 | solution.py:48
  264.6 9.5 %convolution_bitcast_fusion = f32[1280,128]{0,1:T(8,128)} fusion(f32[1280,1280]{1,0:T(8,128)} %get-tuple-element.463, f32[1280,128]{1,0:T(8,128)S(1)} %copy.20, f32[1280,128]{1,0:T(8,128)S(1)} %copy.21, f32[8,1280,128]{2,1,0:T(8,128)} %get-tuple-element.460, s32[]{:T(128)S(6)} %select_n.86), kind=kOutput, calls=%fused_computation.1 | convolution fusion | flops 2517073920 | bytes 9175044 | tf_op jit(solution)/shard_map/while/body/eval_jaxpr/cond/branch_1_fun/dot_general | solution.py:37
  274.1 3.1 dynamic_update_slice.7
  280.4 12.3 %collective-permute-done = f32[1280,128]{0,1:T(8,128)S(1)} collective-permute-done((f32[1280,128]{0,1:T(8,128)}, f32[1280,128]{0,1:T(8,128)S(1)}, u32[]{:S(2)}, u32[]{:S(2)}) %collective-permute-start) | collective-permute-done | bytes 655392 | tf_op jit(solution)/shard_map/while/body/eval_jaxpr/ppermute | solution.py:10
  292.7 16.3 %conditional.2 = (f32[1280,128]{0,1:T(8,128)}, f32[1280,1024]{0,1:T(8,128)}) conditional(s32[]{:T(128)} %convert_element_type.11, f32[1280,1024]{0,1:T(8,128)} %get-tuple-element.579, (s32[]{:T(128)}, pred[]{:T(512)}, pred[]{:T(512)}, s32[]{:T(128)}, s32[8,11]{1,0:T(8,128)}, /*index=5*/s32[]{:T(128)}, f32[8,1280,128]{2,1,0:T(8,128)}, ...), branch_computations={%region_1.1_spmd, %region_2.2_spmd.clone} | conditional | flops 2517073920 | bytes 13107479 | solution.py:48
  296.4 9.5 %convolution_bitcast_fusion = f32[1280,128]{0,1:T(8,128)} fusion(f32[1280,1280]{1,0:T(8,128)} %get-tuple-element.463, f32[1280,128]{1,0:T(8,128)S(1)} %copy.20, f32[1280,128]{1,0:T(8,128)S(1)} %copy.21, f32[8,1280,128]{2,1,0:T(8,128)} %get-tuple-element.460, s32[]{:T(128)S(6)} %select_n.86), kind=kOutput, calls=%fused_computation.1 | convolution fusion | flops 2517073920 | bytes 9175044 | tf_op jit(solution)/shard_map/while/body/eval_jaxpr/cond/branch_1_fun/dot_general | solution.py:37
  305.8 3.1 dynamic_update_slice.7
  312.2 12.3 %collective-permute-done = f32[1280,128]{0,1:T(8,128)S(1)} collective-permute-done((f32[1280,128]{0,1:T(8,128)}, f32[1280,128]{0,1:T(8,128)S(1)}, u32[]{:S(2)}, u32[]{:S(2)}) %collective-permute-start) | collective-permute-done | bytes 655392 | tf_op jit(solution)/shard_map/while/body/eval_jaxpr/ppermute | solution.py:10
  324.4 16.3 %conditional.2 = (f32[1280,128]{0,1:T(8,128)}, f32[1280,1024]{0,1:T(8,128)}) conditional(s32[]{:T(128)} %convert_element_type.11, f32[1280,1024]{0,1:T(8,128)} %get-tuple-element.579, (s32[]{:T(128)}, pred[]{:T(512)}, pred[]{:T(512)}, s32[]{:T(128)}, s32[8,11]{1,0:T(8,128)}, /*index=5*/s32[]{:T(128)}, f32[8,1280,128]{2,1,0:T(8,128)}, ...), branch_computations={%region_1.1_spmd, %region_2.2_spmd.clone} | conditional | flops 2517073920 | bytes 13107479 | solution.py:48
  328.1 9.5 %convolution_bitcast_fusion = f32[1280,128]{0,1:T(8,128)} fusion(f32[1280,1280]{1,0:T(8,128)} %get-tuple-element.463, f32[1280,128]{1,0:T(8,128)S(1)} %copy.20, f32[1280,128]{1,0:T(8,128)S(1)} %copy.21, f32[8,1280,128]{2,1,0:T(8,128)} %get-tuple-element.460, s32[]{:T(128)S(6)} %select_n.86), kind=kOutput, calls=%fused_computation.1 | convolution fusion | flops 2517073920 | bytes 9175044 | tf_op jit(solution)/shard_map/while/body/eval_jaxpr/cond/branch_1_fun/dot_general | solution.py:37
  337.6 3.1 dynamic_update_slice.7
  343.9 12.3 %collective-permute-done = f32[1280,128]{0,1:T(8,128)S(1)} collective-permute-done((f32[1280,128]{0,1:T(8,128)}, f32[1280,128]{0,1:T(8,128)S(1)}, u32[]{:S(2)}, u32[]{:S(2)}) %collective-permute-start) | collective-permute-done | bytes 655392 | tf_op jit(solution)/shard_map/while/body/eval_jaxpr/ppermute | solution.py:10
  356.2 16.3 %conditional.2 = (f32[1280,128]{0,1:T(8,128)}, f32[1280,1024]{0,1:T(8,128)}) conditional(s32[]{:T(128)} %convert_element_type.11, f32[1280,1024]{0,1:T(8,128)} %get-tuple-element.579, (s32[]{:T(128)}, pred[]{:T(512)}, pred[]{:T(512)}, s32[]{:T(128)}, s32[8,11]{1,0:T(8,128)}, /*index=5*/s32[]{:T(128)}, f32[8,1280,128]{2,1,0:T(8,128)}, ...), branch_computations={%region_1.1_spmd, %region_2.2_spmd.clone} | conditional | flops 2517073920 | bytes 13107479 | solution.py:48
  359.9 9.5 %convolution_bitcast_fusion = f32[1280,128]{0,1:T(8,128)} fusion(f32[1280,1280]{1,0:T(8,128)} %get-tuple-element.463, f32[1280,128]{1,0:T(8,128)S(1)} %copy.20, f32[1280,128]{1,0:T(8,128)S(1)} %copy.21, f32[8,1280,128]{2,1,0:T(8,128)} %get-tuple-element.460, s32[]{:T(128)S(6)} %select_n.86), kind=kOutput, calls=%fused_computation.1 | convolution fusion | flops 2517073920 | bytes 9175044 | tf_op jit(solution)/shard_map/while/body/eval_jaxpr/cond/branch_1_fun/dot_general | solution.py:37
  369.4 3.1 dynamic_update_slice.7
  375.7 12.3 %collective-permute-done = f32[1280,128]{0,1:T(8,128)S(1)} collective-permute-done((f32[1280,128]{0,1:T(8,128)}, f32[1280,128]{0,1:T(8,128)S(1)}, u32[]{:S(2)}, u32[]{:S(2)}) %collective-permute-start) | collective-permute-done | bytes 655392 | tf_op jit(solution)/shard_map/while/body/eval_jaxpr/ppermute | solution.py:10
  388.0 16.3 %conditional.2 = (f32[1280,128]{0,1:T(8,128)}, f32[1280,1024]{0,1:T(8,128)}) conditional(s32[]{:T(128)} %convert_element_type.11, f32[1280,1024]{0,1:T(8,128)} %get-tuple-element.579, (s32[]{:T(128)}, pred[]{:T(512)}, pred[]{:T(512)}, s32[]{:T(128)}, s32[8,11]{1,0:T(8,128)}, /*index=5*/s32[]{:T(128)}, f32[8,1280,128]{2,1,0:T(8,128)}, ...), branch_computations={%region_1.1_spmd, %region_2.2_spmd.clone} | conditional | flops 2517073920 | bytes 13107479 | solution.py:48
  391.6 9.5 %convolution_bitcast_fusion = f32[1280,128]{0,1:T(8,128)} fusion(f32[1280,1280]{1,0:T(8,128)} %get-tuple-element.463, f32[1280,128]{1,0:T(8,128)S(1)} %copy.20, f32[1280,128]{1,0:T(8,128)S(1)} %copy.21, f32[8,1280,128]{2,1,0:T(8,128)} %get-tuple-element.460, s32[]{:T(128)S(6)} %select_n.86), kind=kOutput, calls=%fused_computation.1 | convolution fusion | flops 2517073920 | bytes 9175044 | tf_op jit(solution)/shard_map/while/body/eval_jaxpr/cond/branch_1_fun/dot_general | solution.py:37
  401.1 3.1 dynamic_update_slice.7
  407.4 12.3 %collective-permute-done = f32[1280,128]{0,1:T(8,128)S(1)} collective-permute-done((f32[1280,128]{0,1:T(8,128)}, f32[1280,128]{0,1:T(8,128)S(1)}, u32[]{:S(2)}, u32[]{:S(2)}) %collective-permute-start) | collective-permute-done | bytes 655392 | tf_op jit(solution)/shard_map/while/body/eval_jaxpr/ppermute | solution.py:10
  419.7 16.3 %conditional.2 = (f32[1280,128]{0,1:T(8,128)}, f32[1280,1024]{0,1:T(8,128)}) conditional(s32[]{:T(128)} %convert_element_type.11, f32[1280,1024]{0,1:T(8,128)} %get-tuple-element.579, (s32[]{:T(128)}, pred[]{:T(512)}, pred[]{:T(512)}, s32[]{:T(128)}, s32[8,11]{1,0:T(8,128)}, /*index=5*/s32[]{:T(128)}, f32[8,1280,128]{2,1,0:T(8,128)}, ...), branch_computations={%region_1.1_spmd, %region_2.2_spmd.clone} | conditional | flops 2517073920 | bytes 13107479 | solution.py:48
  423.4 9.5 %convolution_bitcast_fusion = f32[1280,128]{0,1:T(8,128)} fusion(f32[1280,1280]{1,0:T(8,128)} %get-tuple-element.463, f32[1280,128]{1,0:T(8,128)S(1)} %copy.20, f32[1280,128]{1,0:T(8,128)S(1)} %copy.21, f32[8,1280,128]{2,1,0:T(8,128)} %get-tuple-element.460, s32[]{:T(128)S(6)} %select_n.86), kind=kOutput, calls=%fused_computation.1 | convolution fusion | flops 2517073920 | bytes 9175044 | tf_op jit(solution)/shard_map/while/body/eval_jaxpr/cond/branch_1_fun/dot_general | solution.py:37
  432.9 3.1 dynamic_update_slice.7
  439.2 12.0 %collective-permute-done = f32[1280,128]{0,1:T(8,128)S(1)} collective-permute-done((f32[1280,128]{0,1:T(8,128)}, f32[1280,128]{0,1:T(8,128)S(1)}, u32[]{:S(2)}, u32[]{:S(2)}) %collective-permute-start) | collective-permute-done | bytes 655392 | tf_op jit(solution)/shard_map/while/body/eval_jaxpr/ppermute | solution.py:10
  451.2 16.0 %conditional.2 = (f32[1280,128]{0,1:T(8,128)}, f32[1280,1024]{0,1:T(8,128)}) conditional(s32[]{:T(128)} %convert_element_type.11, f32[1280,1024]{0,1:T(8,128)} %get-tuple-element.579, (s32[]{:T(128)}, pred[]{:T(512)}, pred[]{:T(512)}, s32[]{:T(128)}, s32[8,11]{1,0:T(8,128)}, /*index=5*/s32[]{:T(128)}, f32[8,1280,128]{2,1,0:T(8,128)}, ...), branch_computations={%region_1.1_spmd, %region_2.2_spmd.clone} | conditional | flops 2517073920 | bytes 13107479 | solution.py:48
  454.9 9.5 %convolution_bitcast_fusion = f32[1280,128]{0,1:T(8,128)} fusion(f32[1280,1280]{1,0:T(8,128)} %get-tuple-element.463, f32[1280,128]{1,0:T(8,128)S(1)} %copy.20, f32[1280,128]{1,0:T(8,128)S(1)} %copy.21, f32[8,1280,128]{2,1,0:T(8,128)} %get-tuple-element.460, s32[]{:T(128)S(6)} %select_n.86), kind=kOutput, calls=%fused_computation.1 | convolution fusion | flops 2517073920 | bytes 9175044 | tf_op jit(solution)/shard_map/while/body/eval_jaxpr/cond/branch_1_fun/dot_general | solution.py:37
  464.4 2.9 dynamic_update_slice.7
  471.5 15.3 %collective-permute-done.1 = f32[1280,128]{0,1:T(8,128)S(1)} collective-permute-done((f32[1280,128]{0,1:T(8,128)}, f32[1280,128]{0,1:T(8,128)S(1)}, u32[]{:S(2)}, u32[]{:S(2)}) %collective-permute-start.1) | collective-permute-done | bytes 655392 | tf_op jit(solution)/shard_map/while/body/eval_jaxpr/ppermute | solution.py:10
  488.9 11.9 %collective-permute-start.1 = (f32[1280,128]{0,1:T(8,128)}, f32[1280,128]{0,1:T(8,128)S(1)}, u32[]{:S(2)}, u32[]{:S(2)}) collective-permute-start(f32[1280,128]{0,1:T(8,128)} %get-tuple-element.556), channel_id=1, source_target_pairs={{0,8},{8,16},{16,24},{1,9},{9,17},{17,25},{2,10},{10,18},{18,26},{... | collective-permute-start | bytes 1966088 | tf_op jit(solution)/shard_map/while/body/eval_jaxpr/ppermute | solution.py:10
  500.8 13.2 %collective-permute-done.1 = f32[1280,128]{0,1:T(8,128)S(1)} collective-permute-done((f32[1280,128]{0,1:T(8,128)}, f32[1280,128]{0,1:T(8,128)S(1)}, u32[]{:S(2)}, u32[]{:S(2)}) %collective-permute-start.1) | collective-permute-done | bytes 655392 | tf_op jit(solution)/shard_map/while/body/eval_jaxpr/ppermute | solution.py:10
  514.1 20.2 %fusion.6 = f32[1024,1024]{0,1:T(8,128)S(1)} fusion(f32[1280,1024]{0,1:T(8,128)} %get-tuple-element.409, f32[1,1,1024,1280]{3,2,1,0:T(8,128)} %param.11), kind=kOutput, calls=%fused_computation.9 | convolution fusion | flops 16106127360 | bytes 14680064 | tf_op jit(solution)/shard_map/dot_general | solution.py:56
  534.3 5.2 copy.18
  539.5 22.2 %gather_fusion = f32[512,2,1024]{2,1,0:T(2,128)} fusion(f32[2,512,1024]{2,0,1:T(2,128)} %copy.18, s32[1024]{0:T(1024)S(1)} %pad_clamp_fusion), kind=kCustom, calls=%fused_computation | custom fusion | bytes 8390656 | tf_op jit(solution)/shard_map/jit(_take)/gather | solution.py:61
  561.7 6.0 select_bitcast_fusion
  567.8 5.9 copy.17
  574.9 99.5 %all-reduce.3.cloned.1.call-done = f32[2,512,1024]{2,0,1:T(2,128)} async-done(((f32[2,512,1024]{2,0,1:T(2,128)}), f32[2,512,1024]{2,0,1:T(2,128)}) %all-reduce.3.cloned.1.call-update) | async-done | bytes 4194320
  (98 shorter events, 74.1 us)
Async XLA Ops:
  7.2 667.2 %all-reduce.3.cloned.1.call-start = ((), (), s32[]{:S(2)}) async-start(), calls=%async_computation | async-start | bytes 8388608
  10.9 4.4 collective-permute-start
  12.2 18.0 %collective-permute-start.1 = (f32[1280,128]{0,1:T(8,128)}, f32[1280,128]{0,1:T(8,128)S(1)}, u32[]{:S(2)}, u32[]{:S(2)}) collective-permute-start(f32[1280,128]{0,1:T(8,128)} %get-tuple-element.556), channel_id=1, source_target_pairs={{0,8},{8,16},{16,24},{1,9},{9,17},{17,25},{2,10},{10,18},{18,26},{... | collective-permute-start | bytes 1966088 | tf_op jit(solution)/shard_map/while/body/eval_jaxpr/ppermute | solution.py:10
  31.0 5.9 collective-permute-start
  32.3 16.5 %collective-permute-start.1 = (f32[1280,128]{0,1:T(8,128)}, f32[1280,128]{0,1:T(8,128)S(1)}, u32[]{:S(2)}, u32[]{:S(2)}) collective-permute-start(f32[1280,128]{0,1:T(8,128)} %get-tuple-element.556), channel_id=1, source_target_pairs={{0,8},{8,16},{16,24},{1,9},{9,17},{17,25},{2,10},{10,18},{18,26},{... | collective-permute-start | bytes 1966088 | tf_op jit(solution)/shard_map/while/body/eval_jaxpr/ppermute | solution.py:10
  49.7 7.3 %collective-permute-start = (f32[1280,128]{0,1:T(8,128)}, f32[1280,128]{0,1:T(8,128)S(1)}, u32[]{:S(2)}, u32[]{:S(2)}) collective-permute-start(f32[1280,128]{0,1:T(8,128)} %get-tuple-element.556), channel_id=1, source_target_pairs={{0,1},{1,2},{2,3},{3,4},{4,5},{5,6},{6,7},{8,9},{9,10},{10,11},{11... | collective-permute-start | bytes 1966088 | tf_op jit(solution)/shard_map/while/body/eval_jaxpr/ppermute | solution.py:10
  51.0 15.0 %collective-permute-start.1 = (f32[1280,128]{0,1:T(8,128)}, f32[1280,128]{0,1:T(8,128)S(1)}, u32[]{:S(2)}, u32[]{:S(2)}) collective-permute-start(f32[1280,128]{0,1:T(8,128)} %get-tuple-element.556), channel_id=1, source_target_pairs={{0,8},{8,16},{16,24},{1,9},{9,17},{17,25},{2,10},{10,18},{18,26},{... | collective-permute-start | bytes 1966088 | tf_op jit(solution)/shard_map/while/body/eval_jaxpr/ppermute | solution.py:10
  66.9 8.8 %collective-permute-start = (f32[1280,128]{0,1:T(8,128)}, f32[1280,128]{0,1:T(8,128)S(1)}, u32[]{:S(2)}, u32[]{:S(2)}) collective-permute-start(f32[1280,128]{0,1:T(8,128)} %get-tuple-element.556), channel_id=1, source_target_pairs={{0,1},{1,2},{2,3},{3,4},{4,5},{5,6},{6,7},{8,9},{9,10},{10,11},{11... | collective-permute-start | bytes 1966088 | tf_op jit(solution)/shard_map/while/body/eval_jaxpr/ppermute | solution.py:10
  68.2 13.5 %collective-permute-start.1 = (f32[1280,128]{0,1:T(8,128)}, f32[1280,128]{0,1:T(8,128)S(1)}, u32[]{:S(2)}, u32[]{:S(2)}) collective-permute-start(f32[1280,128]{0,1:T(8,128)} %get-tuple-element.556), channel_id=1, source_target_pairs={{0,8},{8,16},{16,24},{1,9},{9,17},{17,25},{2,10},{10,18},{18,26},{... | collective-permute-start | bytes 1966088 | tf_op jit(solution)/shard_map/while/body/eval_jaxpr/ppermute | solution.py:10
  82.6 10.3 %collective-permute-start = (f32[1280,128]{0,1:T(8,128)}, f32[1280,128]{0,1:T(8,128)S(1)}, u32[]{:S(2)}, u32[]{:S(2)}) collective-permute-start(f32[1280,128]{0,1:T(8,128)} %get-tuple-element.556), channel_id=1, source_target_pairs={{0,1},{1,2},{2,3},{3,4},{4,5},{5,6},{6,7},{8,9},{9,10},{10,11},{11... | collective-permute-start | bytes 1966088 | tf_op jit(solution)/shard_map/while/body/eval_jaxpr/ppermute | solution.py:10
  83.9 12.4 %collective-permute-start.1 = (f32[1280,128]{0,1:T(8,128)}, f32[1280,128]{0,1:T(8,128)S(1)}, u32[]{:S(2)}, u32[]{:S(2)}) collective-permute-start(f32[1280,128]{0,1:T(8,128)} %get-tuple-element.556), channel_id=1, source_target_pairs={{0,8},{8,16},{16,24},{1,9},{9,17},{17,25},{2,10},{10,18},{18,26},{... | collective-permute-start | bytes 1966088 | tf_op jit(solution)/shard_map/while/body/eval_jaxpr/ppermute | solution.py:10
  97.2 15.2 %collective-permute-start = (f32[1280,128]{0,1:T(8,128)}, f32[1280,128]{0,1:T(8,128)S(1)}, u32[]{:S(2)}, u32[]{:S(2)}) collective-permute-start(f32[1280,128]{0,1:T(8,128)} %get-tuple-element.556), channel_id=1, source_target_pairs={{0,1},{1,2},{2,3},{3,4},{4,5},{5,6},{6,7},{8,9},{9,10},{10,11},{11... | collective-permute-start | bytes 1966088 | tf_op jit(solution)/shard_map/while/body/eval_jaxpr/ppermute | solution.py:10
  98.5 13.9 %collective-permute-start.1 = (f32[1280,128]{0,1:T(8,128)}, f32[1280,128]{0,1:T(8,128)S(1)}, u32[]{:S(2)}, u32[]{:S(2)}) collective-permute-start(f32[1280,128]{0,1:T(8,128)} %get-tuple-element.556), channel_id=1, source_target_pairs={{0,8},{8,16},{16,24},{1,9},{9,17},{17,25},{2,10},{10,18},{18,26},{... | collective-permute-start | bytes 1966088 | tf_op jit(solution)/shard_map/while/body/eval_jaxpr/ppermute | solution.py:10
  113.3 19.0 %collective-permute-start = (f32[1280,128]{0,1:T(8,128)}, f32[1280,128]{0,1:T(8,128)S(1)}, u32[]{:S(2)}, u32[]{:S(2)}) collective-permute-start(f32[1280,128]{0,1:T(8,128)} %get-tuple-element.556), channel_id=1, source_target_pairs={{0,1},{1,2},{2,3},{3,4},{4,5},{5,6},{6,7},{8,9},{9,10},{10,11},{11... | collective-permute-start | bytes 1966088 | tf_op jit(solution)/shard_map/while/body/eval_jaxpr/ppermute | solution.py:10
  114.5 17.7 %collective-permute-start.1 = (f32[1280,128]{0,1:T(8,128)}, f32[1280,128]{0,1:T(8,128)S(1)}, u32[]{:S(2)}, u32[]{:S(2)}) collective-permute-start(f32[1280,128]{0,1:T(8,128)} %get-tuple-element.556), channel_id=1, source_target_pairs={{0,8},{8,16},{16,24},{1,9},{9,17},{17,25},{2,10},{10,18},{18,26},{... | collective-permute-start | bytes 1966088 | tf_op jit(solution)/shard_map/while/body/eval_jaxpr/ppermute | solution.py:10
  133.2 19.0 %collective-permute-start = (f32[1280,128]{0,1:T(8,128)}, f32[1280,128]{0,1:T(8,128)S(1)}, u32[]{:S(2)}, u32[]{:S(2)}) collective-permute-start(f32[1280,128]{0,1:T(8,128)} %get-tuple-element.556), channel_id=1, source_target_pairs={{0,1},{1,2},{2,3},{3,4},{4,5},{5,6},{6,7},{8,9},{9,10},{10,11},{11... | collective-permute-start | bytes 1966088 | tf_op jit(solution)/shard_map/while/body/eval_jaxpr/ppermute | solution.py:10
  134.5 17.7 %collective-permute-start.1 = (f32[1280,128]{0,1:T(8,128)}, f32[1280,128]{0,1:T(8,128)S(1)}, u32[]{:S(2)}, u32[]{:S(2)}) collective-permute-start(f32[1280,128]{0,1:T(8,128)} %get-tuple-element.556), channel_id=1, source_target_pairs={{0,8},{8,16},{16,24},{1,9},{9,17},{17,25},{2,10},{10,18},{18,26},{... | collective-permute-start | bytes 1966088 | tf_op jit(solution)/shard_map/while/body/eval_jaxpr/ppermute | solution.py:10
  153.1 75.9 %collective-permute-start = (f32[1280,128]{0,1:T(8,128)}, f32[1280,128]{0,1:T(8,128)S(1)}, u32[]{:S(2)}, u32[]{:S(2)}) collective-permute-start(f32[1280,128]{0,1:T(8,128)} %get-tuple-element.556), channel_id=1, source_target_pairs={{0,1},{1,2},{2,3},{3,4},{4,5},{5,6},{6,7},{8,9},{9,10},{10,11},{11... | collective-permute-start | bytes 1966088 | tf_op jit(solution)/shard_map/while/body/eval_jaxpr/ppermute | solution.py:10
  154.4 74.7 %collective-permute-start.1 = (f32[1280,128]{0,1:T(8,128)}, f32[1280,128]{0,1:T(8,128)S(1)}, u32[]{:S(2)}, u32[]{:S(2)}) collective-permute-start(f32[1280,128]{0,1:T(8,128)} %get-tuple-element.556), channel_id=1, source_target_pairs={{0,8},{8,16},{16,24},{1,9},{9,17},{17,25},{2,10},{10,18},{18,26},{... | collective-permute-start | bytes 1966088 | tf_op jit(solution)/shard_map/while/body/eval_jaxpr/ppermute | solution.py:10
  245.3 15.6 %collective-permute-start = (f32[1280,128]{0,1:T(8,128)}, f32[1280,128]{0,1:T(8,128)S(1)}, u32[]{:S(2)}, u32[]{:S(2)}) collective-permute-start(f32[1280,128]{0,1:T(8,128)} %get-tuple-element.556), channel_id=1, source_target_pairs={{0,1},{1,2},{2,3},{3,4},{4,5},{5,6},{6,7},{8,9},{9,10},{10,11},{11... | collective-permute-start | bytes 1966088 | tf_op jit(solution)/shard_map/while/body/eval_jaxpr/ppermute | solution.py:10
  246.6 14.3 %collective-permute-start.1 = (f32[1280,128]{0,1:T(8,128)}, f32[1280,128]{0,1:T(8,128)S(1)}, u32[]{:S(2)}, u32[]{:S(2)}) collective-permute-start(f32[1280,128]{0,1:T(8,128)} %get-tuple-element.556), channel_id=1, source_target_pairs={{0,8},{8,16},{16,24},{1,9},{9,17},{17,25},{2,10},{10,18},{18,26},{... | collective-permute-start | bytes 1966088 | tf_op jit(solution)/shard_map/while/body/eval_jaxpr/ppermute | solution.py:10
  277.2 15.5 %collective-permute-start = (f32[1280,128]{0,1:T(8,128)}, f32[1280,128]{0,1:T(8,128)S(1)}, u32[]{:S(2)}, u32[]{:S(2)}) collective-permute-start(f32[1280,128]{0,1:T(8,128)} %get-tuple-element.556), channel_id=1, source_target_pairs={{0,1},{1,2},{2,3},{3,4},{4,5},{5,6},{6,7},{8,9},{9,10},{10,11},{11... | collective-permute-start | bytes 1966088 | tf_op jit(solution)/shard_map/while/body/eval_jaxpr/ppermute | solution.py:10
  278.5 14.2 %collective-permute-start.1 = (f32[1280,128]{0,1:T(8,128)}, f32[1280,128]{0,1:T(8,128)S(1)}, u32[]{:S(2)}, u32[]{:S(2)}) collective-permute-start(f32[1280,128]{0,1:T(8,128)} %get-tuple-element.556), channel_id=1, source_target_pairs={{0,8},{8,16},{16,24},{1,9},{9,17},{17,25},{2,10},{10,18},{18,26},{... | collective-permute-start | bytes 1966088 | tf_op jit(solution)/shard_map/while/body/eval_jaxpr/ppermute | solution.py:10
  308.9 15.5 %collective-permute-start = (f32[1280,128]{0,1:T(8,128)}, f32[1280,128]{0,1:T(8,128)S(1)}, u32[]{:S(2)}, u32[]{:S(2)}) collective-permute-start(f32[1280,128]{0,1:T(8,128)} %get-tuple-element.556), channel_id=1, source_target_pairs={{0,1},{1,2},{2,3},{3,4},{4,5},{5,6},{6,7},{8,9},{9,10},{10,11},{11... | collective-permute-start | bytes 1966088 | tf_op jit(solution)/shard_map/while/body/eval_jaxpr/ppermute | solution.py:10
  310.2 14.2 %collective-permute-start.1 = (f32[1280,128]{0,1:T(8,128)}, f32[1280,128]{0,1:T(8,128)S(1)}, u32[]{:S(2)}, u32[]{:S(2)}) collective-permute-start(f32[1280,128]{0,1:T(8,128)} %get-tuple-element.556), channel_id=1, source_target_pairs={{0,8},{8,16},{16,24},{1,9},{9,17},{17,25},{2,10},{10,18},{18,26},{... | collective-permute-start | bytes 1966088 | tf_op jit(solution)/shard_map/while/body/eval_jaxpr/ppermute | solution.py:10
  340.7 15.5 %collective-permute-start = (f32[1280,128]{0,1:T(8,128)}, f32[1280,128]{0,1:T(8,128)S(1)}, u32[]{:S(2)}, u32[]{:S(2)}) collective-permute-start(f32[1280,128]{0,1:T(8,128)} %get-tuple-element.556), channel_id=1, source_target_pairs={{0,1},{1,2},{2,3},{3,4},{4,5},{5,6},{6,7},{8,9},{9,10},{10,11},{11... | collective-permute-start | bytes 1966088 | tf_op jit(solution)/shard_map/while/body/eval_jaxpr/ppermute | solution.py:10
  342.0 14.2 %collective-permute-start.1 = (f32[1280,128]{0,1:T(8,128)}, f32[1280,128]{0,1:T(8,128)S(1)}, u32[]{:S(2)}, u32[]{:S(2)}) collective-permute-start(f32[1280,128]{0,1:T(8,128)} %get-tuple-element.556), channel_id=1, source_target_pairs={{0,8},{8,16},{16,24},{1,9},{9,17},{17,25},{2,10},{10,18},{18,26},{... | collective-permute-start | bytes 1966088 | tf_op jit(solution)/shard_map/while/body/eval_jaxpr/ppermute | solution.py:10
  372.5 15.5 %collective-permute-start = (f32[1280,128]{0,1:T(8,128)}, f32[1280,128]{0,1:T(8,128)S(1)}, u32[]{:S(2)}, u32[]{:S(2)}) collective-permute-start(f32[1280,128]{0,1:T(8,128)} %get-tuple-element.556), channel_id=1, source_target_pairs={{0,1},{1,2},{2,3},{3,4},{4,5},{5,6},{6,7},{8,9},{9,10},{10,11},{11... | collective-permute-start | bytes 1966088 | tf_op jit(solution)/shard_map/while/body/eval_jaxpr/ppermute | solution.py:10
  373.8 14.2 %collective-permute-start.1 = (f32[1280,128]{0,1:T(8,128)}, f32[1280,128]{0,1:T(8,128)S(1)}, u32[]{:S(2)}, u32[]{:S(2)}) collective-permute-start(f32[1280,128]{0,1:T(8,128)} %get-tuple-element.556), channel_id=1, source_target_pairs={{0,8},{8,16},{16,24},{1,9},{9,17},{17,25},{2,10},{10,18},{18,26},{... | collective-permute-start | bytes 1966088 | tf_op jit(solution)/shard_map/while/body/eval_jaxpr/ppermute | solution.py:10
  404.2 15.5 %collective-permute-start = (f32[1280,128]{0,1:T(8,128)}, f32[1280,128]{0,1:T(8,128)S(1)}, u32[]{:S(2)}, u32[]{:S(2)}) collective-permute-start(f32[1280,128]{0,1:T(8,128)} %get-tuple-element.556), channel_id=1, source_target_pairs={{0,1},{1,2},{2,3},{3,4},{4,5},{5,6},{6,7},{8,9},{9,10},{10,11},{11... | collective-permute-start | bytes 1966088 | tf_op jit(solution)/shard_map/while/body/eval_jaxpr/ppermute | solution.py:10
  405.5 14.2 %collective-permute-start.1 = (f32[1280,128]{0,1:T(8,128)}, f32[1280,128]{0,1:T(8,128)S(1)}, u32[]{:S(2)}, u32[]{:S(2)}) collective-permute-start(f32[1280,128]{0,1:T(8,128)} %get-tuple-element.556), channel_id=1, source_target_pairs={{0,8},{8,16},{16,24},{1,9},{9,17},{17,25},{2,10},{10,18},{18,26},{... | collective-permute-start | bytes 1966088 | tf_op jit(solution)/shard_map/while/body/eval_jaxpr/ppermute | solution.py:10
  436.0 15.3 %collective-permute-start = (f32[1280,128]{0,1:T(8,128)}, f32[1280,128]{0,1:T(8,128)S(1)}, u32[]{:S(2)}, u32[]{:S(2)}) collective-permute-start(f32[1280,128]{0,1:T(8,128)} %get-tuple-element.556), channel_id=1, source_target_pairs={{0,1},{1,2},{2,3},{3,4},{4,5},{5,6},{6,7},{8,9},{9,10},{10,11},{11... | collective-permute-start | bytes 1966088 | tf_op jit(solution)/shard_map/while/body/eval_jaxpr/ppermute | solution.py:10
  437.3 14.0 %collective-permute-start.1 = (f32[1280,128]{0,1:T(8,128)}, f32[1280,128]{0,1:T(8,128)S(1)}, u32[]{:S(2)}, u32[]{:S(2)}) collective-permute-start(f32[1280,128]{0,1:T(8,128)} %get-tuple-element.556), channel_id=1, source_target_pairs={{0,8},{8,16},{16,24},{1,9},{9,17},{17,25},{2,10},{10,18},{18,26},{... | collective-permute-start | bytes 1966088 | tf_op jit(solution)/shard_map/while/body/eval_jaxpr/ppermute | solution.py:10
  467.3 4.2 collective-permute-start
  468.6 18.2 %collective-permute-start.1 = (f32[1280,128]{0,1:T(8,128)}, f32[1280,128]{0,1:T(8,128)S(1)}, u32[]{:S(2)}, u32[]{:S(2)}) collective-permute-start(f32[1280,128]{0,1:T(8,128)} %get-tuple-element.556), channel_id=1, source_target_pairs={{0,8},{8,16},{16,24},{1,9},{9,17},{17,25},{2,10},{10,18},{18,26},{... | collective-permute-start | bytes 1966088 | tf_op jit(solution)/shard_map/while/body/eval_jaxpr/ppermute | solution.py:10
  487.6 13.2 %collective-permute-start = (f32[1280,128]{0,1:T(8,128)}, f32[1280,128]{0,1:T(8,128)S(1)}, u32[]{:S(2)}, u32[]{:S(2)}) collective-permute-start(f32[1280,128]{0,1:T(8,128)} %get-tuple-element.556), channel_id=1, source_target_pairs={{0,1},{1,2},{2,3},{3,4},{4,5},{5,6},{6,7},{8,9},{9,10},{10,11},{11... | collective-permute-start | bytes 1966088 | tf_op jit(solution)/shard_map/while/body/eval_jaxpr/ppermute | solution.py:10
  488.9 25.2 %collective-permute-start.1 = (f32[1280,128]{0,1:T(8,128)}, f32[1280,128]{0,1:T(8,128)S(1)}, u32[]{:S(2)}, u32[]{:S(2)}) collective-permute-start(f32[1280,128]{0,1:T(8,128)} %get-tuple-element.556), channel_id=1, source_target_pairs={{0,8},{8,16},{16,24},{1,9},{9,17},{17,25},{2,10},{10,18},{18,26},{... | collective-permute-start | bytes 1966088 | tf_op jit(solution)/shard_map/while/body/eval_jaxpr/ppermute | solution.py:10
  534.2 5.3 copy-start
  567.8 5.9 copy-start.1
Sparse Core Ops, SparseCore 0:
  567.9 106.4 all-reduce.2
where the time goes:
time: 688 us; the launch traced here: 684 us
  waiting for transfers between devices  395 us (57%)
  matrix products  96 us (14%)
  local copies, waits for them, and re-layouts  86.3 us (13%)
  starting transfers between devices  69.1 us (10%)
  loops' own time  16.1 us (2%)
  between operations  14.7 us (2%)
    ppermute x36, waiting for transfers between devices, passed_along(): lax.ppermute(value, axis, [(source, source + steps) for source in range(f...  296 us
    unnamed x2, waiting for transfers between devices  99.5 us
    dot_general x8, matrix products, work(): jnp.dot(operator, inflow, precision=lax.Precision.HIGHEST, preferred_elem...  75.9 us
    ppermute x36, starting transfers between devices, passed_along(): lax.ppermute(value, axis, [(source, source + steps) for source in range(f...  69.1 us
    dynamic_update_slice x8, local copies, waits for them, and re-layouts, work(): return (result, lax.dynamic_update_slice_in_dim(stored, result, start, 1))  24.5 us
    gather x1, local copies, waits for them, and re-layouts, local(): ordered = jnp.take(partial_value, owner_map[0], axis=1)  22.2 us
    dot_general x1, matrix products, local(): jnp.dot(probe[0, 0], traces, precision=lax.Precision.HIGHEST, preferred_e...  20.2 us
    another operation x18, loops' own time, advance(): result, traces = lax.cond(active, work, skip, traces)  15.7 us
  transfers between devices with their start and end apart: 37, of which 24 were waited for; matrix products, arithmetic and copies ran while one was open for 1% of the time, Pallas kernels for 0%

commit v1 on v0

v1 whole, which is shorter than its diff:
```python
import functools

import jax
import jax.numpy as jnp
from jax import lax
from jax.experimental import pallas as pl
from jax.experimental.pallas import tpu as pltpu
from jax.sharding import PartitionSpec as P

MESH = pl.DeviceIdType.MESH
SPLITS = 2
BLOCKS = 2


def divided(value):
    high = value.astype(jnp.bfloat16).astype(jnp.float32)
    return high, value - high


def kernel(
    cols,
    rows,
    pick_ref,
    owner_ref,
    sources_hbm,
    green_hbm,
    probe_hbm,
    traces_hbm,
    data_hbm,
    sources,
    staging,
    operator,
    receive_map,
    inflow,
    stacked,
    wide,
    traces,
    outbox,
    upper,
    lefter,
    partial,
    *rest,
):
    stages = cols.bit_length() - 1
    arrivals = rest[:stages]
    (
        green_sem,
        sources_sem,
        probe_sem,
        down_sem,
        right_sem,
        upper_sem,
        lefter_sem,
        traces_sem,
        data_sem,
        sum_send_sem,
        sum_recv_sem,
    ) = rest[stages:]
    row = lax.axis_index("gz")
    col = lax.axis_index("gx")
    diag = row + col
    trace = green_hbm.shape[0]
    shots = sources_hbm.shape[2]
    window = pick_ref.shape[0]
    half = trace // SPLITS
    piece = half // BLOCKS
    share = shots // SPLITS
    receivers = owner_ref.shape[1]
    owned = receivers // cols

    loads = []
    for block in range(BLOCKS):
        for side in range(SPLITS):
            where = pl.ds(side * half + block * piece, piece)
            loads.append(
                pltpu.make_async_copy(
                    green_hbm.at[where], staging.at[where], green_sem.at[block * SPLITS + side]
                )
            )
    for load in loads:
        load.start()
    sources_load = pltpu.make_async_copy(sources_hbm, sources, sources_sem)
    sources_load.start()

    partners = [col ^ (cols >> (stage + 1)) for stage in range(stages)]
    barrier = pltpu.get_barrier_semaphore()

    @pl.when(row > 0)
    def _():
        pl.semaphore_signal(barrier, inc=1, device_id={"gz": row - 1}, device_id_type=MESH)

    @pl.when(row < rows - 1)
    def _():
        pl.semaphore_signal(barrier, inc=1, device_id={"gz": row + 1}, device_id_type=MESH)

    for offset in range(1, cols):
        other = lax.rem(col + offset, cols)
        pl.semaphore_signal(barrier, inc=1, device_id={"gx": other}, device_id_type=MESH)

    for block in range(BLOCKS):
        for side in range(SPLITS):
            loads[block * SPLITS + side].wait()
            high, low = divided(staging[pl.ds(side * half + block * piece, piece), :])
            place = pl.ds((block * SPLITS + side) * piece, piece)
            operator[place, :trace] = high.astype(jnp.bfloat16)
            operator[place, trace:] = low.astype(jnp.bfloat16)
    probe_load = pltpu.make_async_copy(
        probe_hbm, staging.at[pl.ds(0, SPLITS * receivers)], probe_sem
    )
    probe_load.start()
    sources_load.wait()

    peers = cols - 1 + (row > 0).astype(jnp.int32) + (row < rows - 1).astype(jnp.int32)
    pl.semaphore_wait(barrier, peers)

    def downward(slot, part):
        return pltpu.make_async_remote_copy(
            src_ref=outbox.at[slot, part],
            dst_ref=upper.at[slot, part],
            send_sem=down_sem.at[slot],
            recv_sem=upper_sem.at[slot],
            device_id={"gz": lax.rem(row + 1, rows)},
            device_id_type=MESH,
        )

    def rightward(slot, part):
        return pltpu.make_async_remote_copy(
            src_ref=outbox.at[slot, part],
            dst_ref=lefter.at[slot, part],
            send_sem=right_sem.at[slot],
            recv_sem=lefter_sem.at[slot],
            device_id={"gx": lax.rem(col + 1, cols)},
            device_id_type=MESH,
        )

    whole = pl.ds(0, half)
    first_lanes = lax.broadcasted_iota(jnp.int32, (half, shots), 1) < share
    piece_lanes = lax.broadcasted_iota(jnp.int32, (piece, shots), 1) < share
    last = window * SPLITS - 1

    def chunk(batch, part):
        slot = batch * SPLITS + part
        chosen = pick_ref[batch, diag]
        top = sources[chosen, :half, :]
        bottom = sources[chosen, half:, :]
        if part == 0:
            inflow[...] = jnp.where(first_lanes, top, pltpu.roll(bottom, share, 1))
        else:
            inflow[...] = jnp.where(first_lanes, pltpu.roll(top, share, 1), bottom)

        @pl.when(row > 0)
        def _():
            downward(slot, whole).wait_recv()
            inflow[...] += 0.5 * upper[slot]

        @pl.when(col > 0)
        def _():
            rightward(slot, whole).wait_recv()
            inflow[...] += 0.5 * lefter[slot]

        high, low = divided(inflow[...])
        top = jnp.where(first_lanes, high, pltpu.roll(low, share, 1)).astype(jnp.bfloat16)
        bottom = jnp.where(first_lanes, pltpu.roll(high, share, 1), low).astype(jnp.bfloat16)
        for copy in range(2):
            stacked[copy * trace : copy * trace + half, :] = top
            stacked[copy * trace + half : (copy + 1) * trace, :] = bottom
        for block in range(BLOCKS):
            result = jnp.dot(
                operator[block * SPLITS * piece : (block + 1) * SPLITS * piece, :],
                stacked[...],
                preferred_element_type=jnp.float32,
            )
            result = result + pltpu.roll(result, share, 1)
            upside, downside = result[:piece], result[piece:]
            area = pl.ds(block * piece, piece)
            outbox[slot, area, :] = jnp.where(piece_lanes, upside, downside)

            @pl.when(row < rows - 1)
            def _():
                downward(slot, area).start()

            @pl.when(col < cols - 1)
            def _():
                rightward(slot, area).start()

            for side, value in ((0, upside), (1, downside)):
                begin = side * half + block * piece
                if part > 0:
                    value = jnp.where(piece_lanes, traces[batch, begin : begin + piece, :], value)
                traces[batch, begin : begin + piece, :] = value

    def traces_out(batch):
        return pltpu.make_async_copy(
            traces.at[batch],
            traces_hbm.at[:, pl.ds(pl.multiple_of(batch * shots, shots), shots)],
            traces_sem.at[batch],
        )

    def arrange_map():
        probe_load.wait()
        spots = lax.broadcasted_iota(jnp.int32, (receivers, receivers), 0)
        chosen = (spots == owner_ref[...]).astype(jnp.float32)
        chosen = jnp.transpose(chosen).astype(jnp.bfloat16)
        for part in range(2):
            values = staging[part * receivers : (part + 1) * receivers, :]
            for index, value in enumerate(divided(values)):
                moved = jnp.dot(
                    chosen, value.astype(jnp.bfloat16), preferred_element_type=jnp.float32
                ).astype(jnp.bfloat16)
                for owner in range(cols):
                    begin = (owner * 2 + part) * owned
                    receive_map[begin : begin + owned, index * trace : (index + 1) * trace] = moved[
                        owner * owned : (owner + 1) * owned
                    ]

    def measure(batch):
        high, low = divided(traces[batch])
        for copy in range(2):
            wide[copy * trace : (copy + 1) * trace, :shots] = high.astype(jnp.bfloat16)
            wide[copy * trace : (copy + 1) * trace, shots:] = low.astype(jnp.bfloat16)
        for side in range(2):
            value = jnp.dot(
                receive_map[side * receivers : (side + 1) * receivers, :],
                wide[...],
                preferred_element_type=jnp.float32,
            )
            partial[batch, side * receivers : (side + 1) * receivers, :] = (
                value[:, :shots] + value[:, shots:]
            )

    def exchange(stage, batch):
        extent = (cols >> (stage + 1)) * 2 * owned
        base = (col // (cols >> stage)) * (cols >> stage) * 2 * owned
        upside = (col // (cols >> (stage + 1))) % 2
        mine = pl.multiple_of(base + upside * extent, 2 * owned)
        theirs = pl.multiple_of(base + (1 - upside) * extent, 2 * owned)
        copy = pltpu.make_async_remote_copy(
            src_ref=partial.at[batch, pl.ds(theirs, extent)],
            dst_ref=arrivals[stage].at[batch],
            send_sem=sum_send_sem.at[stage, batch],
            recv_sem=sum_recv_sem.at[stage, batch],
            device_id={"gx": partners[stage]},
            device_id_type=MESH,
        )
        return copy, pl.ds(mine, extent)

    def data_out(batch, part):
        begin = pl.multiple_of(col * 2 * owned + part * owned, owned)
        return pltpu.make_async_copy(
            partial.at[batch, pl.ds(begin, owned)],
            data_hbm.at[part, :, pl.ds(pl.multiple_of(batch * shots, shots), shots)],
            data_sem.at[batch, part],
        )

    lags = []
    lag = 0
    longest = 0
    for stage in range(stages):
        distance = cols >> (stage + 1)
        upside = (col // distance) % 2
        lag = lag + (1 - upside) * ((distance + 2) // 2)
        longest += (distance + 2) // 2
        lags.append(lag)

    def advance(step, carry):
        @pl.when(step < window)
        def _():
            for part in range(SPLITS):
                chunk(step, part)
            traces_out(step).start()

            @pl.when(step == 0)
            def _():
                arrange_map()

            measure(step)
            exchange(0, step)[0].start()

        for stage in range(stages):
            batch = step - lags[stage]

            @pl.when(jnp.logical_and(batch >= 0, batch < window))
            def _():
                copy, mine = exchange(stage, batch)
                copy.wait_recv()
                partial[batch, mine, :] += arrivals[stage][batch]
                if stage < stages - 1:
                    exchange(stage + 1, batch)[0].start()
                else:
                    for part in range(2):
                        data_out(batch, part).start()

        return carry

    lax.fori_loop(0, window + longest, advance, 0)

    def finish(batch, carry):
        for part in range(SPLITS):
            slot = batch * SPLITS + part

            @pl.when(row < rows - 1)
            def _():
                downward(slot, whole).wait_send()

            @pl.when(col < cols - 1)
            def _():
                rightward(slot, whole).wait_send()

        for stage in range(stages):
            exchange(stage, batch)[0].wait_send()
        traces_out(batch).wait()
        for part in range(2):
            data_out(batch, part).wait()
        return carry

    lax.fori_loop(0, window, finish, 0)


def local(sources, green, probe, batch_pick, owner_map):
    cols = lax.axis_size("gx")
    rows = lax.axis_size("gz")
    batches, trace, shots = sources.shape[2:]
    window = batch_pick.shape[0]
    receivers = owner_map.shape[1]
    owned = receivers // cols
    stages = cols.bit_length() - 1
    slots = window * SPLITS
    half = trace // SPLITS
    total = window * shots
    vmem = pltpu.VMEM
    dma = pltpu.SemaphoreType.DMA
    anywhere = pl.BlockSpec(memory_space=pl.ANY)
    traces, data = pl.pallas_call(
        functools.partial(kernel, cols, rows),
        out_shape=(
            jax.ShapeDtypeStruct((trace, total), jnp.float32),
            jax.ShapeDtypeStruct((2, owned, total), jnp.float32),
        ),
        in_specs=[
            pl.BlockSpec(memory_space=pltpu.SMEM),
            pl.BlockSpec(memory_space=pltpu.VMEM),
            anywhere,
            anywhere,
            anywhere,
        ],
        out_specs=(anywhere, anywhere),
        scratch_shapes=[
            vmem((batches, trace, shots), jnp.float32),
            vmem((max(trace, 2 * receivers), trace), jnp.float32),
            vmem((trace, 2 * trace), jnp.bfloat16),
            vmem((2 * receivers, 2 * trace), jnp.bfloat16),
            vmem((half, shots), jnp.float32),
            vmem((2 * trace, shots), jnp.bfloat16),
            vmem((2 * trace, 2 * shots), jnp.bfloat16),
            vmem((window, trace, shots), jnp.float32),
            vmem((slots, half, shots), jnp.float32),
            vmem((slots, half, shots), jnp.float32),
            vmem((slots, half, shots), jnp.float32),
            vmem((window, 2 * receivers, shots), jnp.float32),
        ]
        + [
            vmem((window, (cols >> (stage + 1)) * 2 * owned, shots), jnp.float32)
            for stage in range(stages)
        ]
        + [
            dma((SPLITS * BLOCKS,)),
            dma(()),
            dma(()),
            dma((slots,)),
            dma((slots,)),
            dma((slots,)),
            dma((slots,)),
            dma((window,)),
            dma((window, 2)),
            dma((stages, window)),
            dma((stages, window)),
        ],
        compiler_params=pltpu.CompilerParams(
            collective_id=0, has_side_effects=True, vmem_limit_bytes=67043328
        ),
    )(batch_pick, owner_map, sources[0, 0], green[0, 0], probe[0, 0])
    return traces[None, None], data[None]


def solution(mesh):
    return jax.shard_map(
        local,
        mesh=mesh,
        in_specs=(
            P("gz", "gx", None, None, None),
            P("gz", "gx", None, None),
            P("gz", "gx", None, None),
            P(),
            P("gz", None),
        ),
        out_specs=(P("gz", "gx", None, None), P("gz", None, "gx", None)),
        check_vma=False,
    )
```

time: 688 us -> 269 us (0.39)
  waiting for transfers between devices: 395 us -> 0 us
  Pallas kernels: 0 us -> 256 us
  matrix products: 96 us -> 0 us
  local copies, waits for them, and re-layouts: 86.3 us -> 6.76 us
  starting transfers between devices: 69.1 us -> 0 us
  loops' own time: 16.1 us -> 0 us
  between operations: 14.7 us -> 0.65 us
    ppermute x36 -> x0, waiting for transfers between devices: 296 us -> none  [passed_along(): lax.ppermute(value, axis, [(source, source + steps) for source in range(f...]
    pallas_call x0 -> x1, Pallas kernels: none -> 256 us  [local(): pl.pallas_call(functools.partial(kernel, cols, rows), out_shape=(jax.Shap...]
    unnamed x2 -> x0, waiting for transfers between devices: 99.5 us -> none
    dot_general x9 -> x0, matrix products: 96 us -> none  [the longest x8 75.9 us: work(): jnp.dot(operator, inflow, precision=lax.Precision.HIGHEST, preferred_elem...]
    ppermute x36 -> x0, starting transfers between devices: 69.1 us -> none  [passed_along(): lax.ppermute(value, axis, [(source, source + steps) for source in range(f...]
    dynamic_update_slice x8 -> x0, local copies, waits for them, and re-layouts: 24.5 us -> none  [work(): return (result, lax.dynamic_update_slice_in_dim(stored, result, start, 1))]
    gather x1 -> x0, local copies, waits for them, and re-layouts: 22.2 us -> none  [local(): ordered = jnp.take(partial_value, owner_map[0], axis=1)]
    another operation x19 -> x0, loops' own time: 16.1 us -> none  [the longest x18 15.7 us: advance(): result, traces = lax.cond(active, work, skip, traces)]
  transfers between devices with their start and end apart: 37 -> 0, of which waited for: 24 -> 0; matrix products, arithmetic and copies ran while one was open for 1% -> 0% of each run, Pallas kernels for 0% -> 0%
where the time goes in v1:
time: 269 us; the launch traced here: 263 us
  Pallas kernels  256 us (95%)
  local copies, waits for them, and re-layouts  6.76 us (3%)
    pallas_call x1, Pallas kernels, local(): pl.pallas_call(functools.partial(kernel, cols, rows), out_shape=(jax.Shap...  256 us
    unnamed x4, local copies, waits for them, and re-layouts  6.76 us

profile of v1, /device:TPU:29, one launch (start us, length us, event | category | flops | bytes accessed | tf_op | source)
XLA Modules:
  0.0 263.3 jit_solution(603349785358876405)
XLA Ops:
  0.6 255.9 %shard_map.68 = (f32[1280,1024]{1,0:T(8,128)}, f32[2,128,1024]{2,1,0:T(8,128)}) custom-call(s32[8,11]{1,0:T(8,128)} %pick_ref.1, s32[1,512]{1,0:T(1,128)} %owner_ref.1, f32[8,1280,128]{2,1,0:T(8,128)} %bitcast.6, f32[1280,1280]{1,0:T(8,128)} %bitcast.5, f32[1024,1280]{1,0:T(8,128)} %bitcast.7), custom_call_target="tpu_custom_call" | custom-call | tf_op jit(solution)/shard_map/pallas_call | solution.py:333
  256.6 0.0 copy-start
  256.6 5.8 %copy.9 = f32[1,1,1280,1024]{3,2,1,0:T(8,128)} copy(f32[1,1,1280,1024]{3,2,1,0:T(8,128)} %bitcast.8) | data formatting | bytes 10485760
  262.4 0.0 copy-done
  262.4 1.0 copy.10
Async XLA Ops:
  256.6 5.8 %copy-start = (f32[2,128,1024]{2,1,0:T(8,128)S(1)}, f32[2,128,1024]{2,1,0:T(8,128)}, u32[]{:S(2)}) copy-start(f32[2,128,1024]{2,1,0:T(8,128)} %get-tuple-element.5) | copy-start | bytes 3145732

commit v2 on v1

--- a/solution.py
+++ b/solution.py
@@ -9,7 +9,7 @@
 
 MESH = pl.DeviceIdType.MESH
 SPLITS = 2
-BLOCKS = 2
+BLOCKS = 4
 
 
 def divided(value):
@@ -41,8 +41,10 @@
     partial,
     *rest,
 ):
-    stages = cols.bit_length() - 1
-    arrivals = rest[:stages]
+    group = cols // 2
+    stages = group.bit_length() - 1
+    crossed = rest[:2]
+    arrivals = (rest[2 : 2 + stages], rest[2 + stages : 2 + 2 * stages])
     (
         green_sem,
         sources_sem,
@@ -53,9 +55,11 @@
         lefter_sem,
         traces_sem,
         data_sem,
+        cross_send_sem,
+        cross_recv_sem,
         sum_send_sem,
         sum_recv_sem,
-    ) = rest[stages:]
+    ) = rest[2 + 2 * stages :]
     row = lax.axis_index("gz")
     col = lax.axis_index("gx")
     diag = row + col
@@ -82,7 +86,6 @@
     sources_load = pltpu.make_async_copy(sources_hbm, sources, sources_sem)
     sources_load.start()
 
-    partners = [col ^ (cols >> (stage + 1)) for stage in range(stages)]
     barrier = pltpu.get_barrier_semaphore()
 
     @pl.when(row > 0)
@@ -228,21 +231,40 @@
                 value[:, :shots] + value[:, shots:]
             )
 
-    def exchange(stage, batch):
-        extent = (cols >> (stage + 1)) * 2 * owned
-        base = (col // (cols >> stage)) * (cols >> stage) * 2 * owned
-        upside = (col // (cols >> (stage + 1))) % 2
-        mine = pl.multiple_of(base + upside * extent, 2 * owned)
-        theirs = pl.multiple_of(base + (1 - upside) * extent, 2 * owned)
+    unit = 2 * owned
+    upside = col // group
+    place = lax.rem(col, group)
+
+    def cross(kind, batch):
+        if kind == 0:
+            area = pl.ds(0, group * unit)
+        else:
+            area = pl.ds(pl.multiple_of((group + place) * unit, unit), unit)
         copy = pltpu.make_async_remote_copy(
-            src_ref=partial.at[batch, pl.ds(theirs, extent)],
-            dst_ref=arrivals[stage].at[batch],
-            send_sem=sum_send_sem.at[stage, batch],
-            recv_sem=sum_recv_sem.at[stage, batch],
-            device_id={"gx": partners[stage]},
+            src_ref=partial.at[batch, area],
+            dst_ref=crossed[kind].at[batch],
+            send_sem=cross_send_sem.at[kind, batch],
+            recv_sem=cross_recv_sem.at[kind, batch],
+            device_id={"gx": lax.rem(col + group, cols)},
             device_id_type=MESH,
         )
-        return copy, pl.ds(mine, extent)
+        return copy, area
+
+    def exchange(kind, stage, batch):
+        distance = group >> (stage + 1)
+        base = kind * group + (place // (2 * distance)) * (2 * distance)
+        bit = lax.rem(place // distance, 2)
+        mine = pl.multiple_of((base + bit * distance) * unit, unit)
+        theirs = pl.multiple_of((base + (1 - bit) * distance) * unit, unit)
+        copy = pltpu.make_async_remote_copy(
+            src_ref=partial.at[batch, pl.ds(theirs, distance * unit)],
+            dst_ref=arrivals[kind][stage].at[batch],
+            send_sem=sum_send_sem.at[kind, stage, batch],
+            recv_sem=sum_recv_sem.at[kind, stage, batch],
+            device_id={"gx": col + (1 - 2 * bit) * distance},
+            device_id_type=MESH,
+        )
+        return copy, pl.ds(mine, distance * unit)
 
     def data_out(batch, part):
         begin = pl.multiple_of(col * 2 * owned + part * owned, owned)
@@ -252,16 +274,6 @@
             data_sem.at[batch, part],
         )
 
-    lags = []
-    lag = 0
-    longest = 0
-    for stage in range(stages):
-        distance = cols >> (stage + 1)
-        upside = (col // distance) % 2
-        lag = lag + (1 - upside) * ((distance + 2) // 2)
-        longest += (distance + 2) // 2
-        lags.append(lag)
-
     def advance(step, carry):
         @pl.when(step < window)
         def _():
@@ -274,25 +286,74 @@
                 arrange_map()
 
             measure(step)
-            exchange(0, step)[0].start()
+
+            @pl.when(upside == 1)
+            def _():
+                cross(0, step)[0].start()
+
+        def sum_out(batch):
+            for part in range(2):
+                data_out(batch, part).start()
+
+        def follow(kind, stage, batch):
+            if stage < stages:
+                exchange(kind, stage, batch)[0].start()
+            elif kind == 0:
+                sum_out(batch)
+            else:
+
+                @pl.when(upside == 0)
+                def _():
+                    cross(1, batch)[0].start()
+
+        def collect(kind, stage, batch):
+            copy, mine = exchange(kind, stage, batch)
+            copy.wait_recv()
+            partial[batch, mine, :] += arrivals[kind][stage][batch]
+            follow(kind, stage + 1, batch)
+
+        @pl.when(step == window)
+        def _():
+            lax.fori_loop(0, window, lambda batch, none: (follow(1, 0, batch), none)[1], 0)
+
+        def within(batch, *more):
+            known = jnp.logical_and(batch >= 0, batch < window)
+            for condition in more:
+                known = jnp.logical_and(known, condition)
+            return known
+
+        early = step - window
+
+        @pl.when(within(early, upside == 0))
+        def _():
+            copy, area = cross(0, early)
+            copy.wait_recv()
+            partial[early, area, :] += crossed[0][early]
+            follow(0, 0, early)
 
         for stage in range(stages):
-            batch = step - lags[stage]
-
-            @pl.when(jnp.logical_and(batch >= 0, batch < window))
-            def _():
-                copy, mine = exchange(stage, batch)
-                copy.wait_recv()
-                partial[batch, mine, :] += arrivals[stage][batch]
-                if stage < stages - 1:
-                    exchange(stage + 1, batch)[0].start()
-                else:
-                    for part in range(2):
-                        data_out(batch, part).start()
+            batch = step - window - 2 - stage
+
+            @pl.when(within(batch))
+            def _():
+                collect(1, stage, batch)
+
+            @pl.when(within(batch, upside == 0))
+            def _():
+                collect(0, stage, batch)
+
+        late = step - window - 3 - stages
+
+        @pl.when(within(late, upside == 1))
+        def _():
+            copy, area = cross(1, late)
+            copy.wait_recv()
+            partial[late, area, :] += crossed[1][late]
+            sum_out(late)
 
         return carry
 
-    lax.fori_loop(0, window + longest, advance, 0)
+    lax.fori_loop(0, 2 * window + stages + 3, advance, 0)
 
     def finish(batch, carry):
         for part in range(SPLITS):
@@ -306,8 +367,18 @@
             def _():
                 rightward(slot, whole).wait_send()
 
+        @pl.when(upside == 1)
+        def _():
+            cross(0, batch)[0].wait_send()
+
+        @pl.when(upside == 0)
+        def _():
+            cross(1, batch)[0].wait_send()
+            for stage in range(stages):
+                exchange(0, stage, batch)[0].wait_send()
+
         for stage in range(stages):
-            exchange(stage, batch)[0].wait_send()
+            exchange(1, stage, batch)[0].wait_send()
         traces_out(batch).wait()
         for part in range(2):
             data_out(batch, part).wait()
@@ -323,7 +394,8 @@
     window = batch_pick.shape[0]
     receivers = owner_map.shape[1]
     owned = receivers // cols
-    stages = cols.bit_length() - 1
+    group = cols // 2
+    stages = group.bit_length() - 1
     slots = window * SPLITS
     half = trace // SPLITS
     total = window * shots
@@ -359,7 +431,12 @@
             vmem((window, 2 * receivers, shots), jnp.float32),
         ]
         + [
-            vmem((window, (cols >> (stage + 1)) * 2 * owned, shots), jnp.float32)
+            vmem((window, group * 2 * owned, shots), jnp.float32),
+            vmem((window, 2 * owned, shots), jnp.float32),
+        ]
+        + [
+            vmem((window, (group >> (stage + 1)) * 2 * owned, shots), jnp.float32)
+            for kind in range(2)
             for stage in range(stages)
         ]
         + [
@@ -372,8 +449,10 @@
             dma((slots,)),
             dma((window,)),
             dma((window, 2)),
-            dma((stages, window)),
-            dma((stages, window)),
+            dma((2, window)),
+            dma((2, window)),
+            dma((2, max(stages, 1), window)),
+            dma((2, max(stages, 1), window)),
         ],
         compiler_params=pltpu.CompilerParams(
             collective_id=0, has_side_effects=True, vmem_limit_bytes=67043328

time: 269 us -> 225 us (0.84); the launches traced: 263 us -> 225 us
  Pallas kernels: 256 us -> 217 us
    pallas_call x1, Pallas kernels: 256 us -> 217 us  [local(): pl.pallas_call(functools.partial(kernel, cols, rows), out_shape=(jax.Shap...]
where the time goes in v2:
time: 225 us
  Pallas kernels  217 us (96%)
  local copies, waits for them, and re-layouts  6.76 us (3%)
    pallas_call x1, Pallas kernels, local(): pl.pallas_call(functools.partial(kernel, cols, rows), out_shape=(jax.Shap...  217 us
    unnamed x4, local copies, waits for them, and re-layouts  6.76 us

profile of v2, /device:TPU:29, one launch (start us, length us, event | category | flops | bytes accessed | tf_op | source)
XLA Modules:
  0.0 224.8 jit_solution(4572737812480471109)
XLA Ops:
  0.6 217.4 %shard_map.68 = (f32[1280,1024]{1,0:T(8,128)}, f32[2,128,1024]{2,1,0:T(8,128)}) custom-call(s32[8,11]{1,0:T(8,128)} %pick_ref.1, s32[1,512]{1,0:T(1,128)} %owner_ref.1, f32[8,1280,128]{2,1,0:T(8,128)} %bitcast.6, f32[1280,1280]{1,0:T(8,128)} %bitcast.5, f32[1024,1280]{1,0:T(8,128)} %bitcast.7), custom_call_target="tpu_custom_call" | custom-call | tf_op jit(solution)/shard_map/pallas_call | solution.py:405
  218.0 0.0 copy-start
  218.0 5.8 %copy.9 = f32[1,1,1280,1024]{3,2,1,0:T(8,128)} copy(f32[1,1,1280,1024]{3,2,1,0:T(8,128)} %bitcast.8) | data formatting | bytes 10485760
  223.8 0.0 copy-done
  223.8 1.0 copy.10
Async XLA Ops:
  218.0 5.8 %copy-start = (f32[2,128,1024]{2,1,0:T(8,128)S(1)}, f32[2,128,1024]{2,1,0:T(8,128)}, u32[]{:S(2)}) copy-start(f32[2,128,1024]{2,1,0:T(8,128)} %get-tuple-element.5) | copy-start | bytes 3145732

commit v3 on v2

--- a/solution.py
+++ b/solution.py
@@ -168,11 +168,14 @@
             stacked[copy * trace : copy * trace + half, :] = top
             stacked[copy * trace + half : (copy + 1) * trace, :] = bottom
         for block in range(BLOCKS):
-            result = jnp.dot(
-                operator[block * SPLITS * piece : (block + 1) * SPLITS * piece, :],
-                stacked[...],
-                preferred_element_type=jnp.float32,
-            )
+            lines = slice(block * SPLITS * piece, (block + 1) * SPLITS * piece)
+            result = 0.0
+            for begin in range(0, 2 * trace, half):
+                result = result + jnp.dot(
+                    operator[lines, begin : begin + half],
+                    stacked[begin : begin + half],
+                    preferred_element_type=jnp.float32,
+                )
             result = result + pltpu.roll(result, share, 1)
             upside, downside = result[:piece], result[piece:]
             area = pl.ds(block * piece, piece)

time: 225 us -> 215 us (0.956)
  Pallas kernels: 217 us -> 208 us
    pallas_call x1, Pallas kernels: 217 us -> 208 us  [local(): pl.pallas_call(functools.partial(kernel, cols, rows), out_shape=(jax.Shap...]
where the time goes in v3:
time: 215 us
  Pallas kernels  208 us (97%)
  local copies, waits for them, and re-layouts  6.76 us (3%)
    pallas_call x1, Pallas kernels, local(): pl.pallas_call(functools.partial(kernel, cols, rows), out_shape=(jax.Shap...  208 us
    unnamed x4, local copies, waits for them, and re-layouts  6.76 us

profile of v3, /device:TPU:29, one launch (start us, length us, event | category | flops | bytes accessed | tf_op | source)
XLA Modules:
  0.0 215.2 jit_solution(4280963759085678341)
XLA Ops:
  0.6 207.8 %shard_map.68 = (f32[1280,1024]{1,0:T(8,128)}, f32[2,128,1024]{2,1,0:T(8,128)}) custom-call(s32[8,11]{1,0:T(8,128)} %pick_ref.1, s32[1,512]{1,0:T(1,128)} %owner_ref.1, f32[8,1280,128]{2,1,0:T(8,128)} %bitcast.6, f32[1280,1280]{1,0:T(8,128)} %bitcast.5, f32[1024,1280]{1,0:T(8,128)} %bitcast.7), custom_call_target="tpu_custom_call" | custom-call | tf_op jit(solution)/shard_map/pallas_call | solution.py:408
  208.4 0.0 copy-start
  208.4 5.8 %copy.9 = f32[1,1,1280,1024]{3,2,1,0:T(8,128)} copy(f32[1,1,1280,1024]{3,2,1,0:T(8,128)} %bitcast.8) | data formatting | bytes 10485760
  214.2 0.0 copy-done
  214.2 1.0 copy.10
Async XLA Ops:
  208.4 5.8 %copy-start = (f32[2,128,1024]{2,1,0:T(8,128)S(1)}, f32[2,128,1024]{2,1,0:T(8,128)}, u32[]{:S(2)}) copy-start(f32[2,128,1024]{2,1,0:T(8,128)} %get-tuple-element.5) | copy-start | bytes 3145732
